TPU v7x, 256 devices: a whole 4x4x8 slice. The times are simulated.
256 devices in a mesh: row: 16 (over x, y), col: 16 (over z, core).
Axes of the slice: x: 4, y: 4, z: 8, core: 2. Of those that a mesh axis runs over, the one named last changes fastest.
Arguments:
- mobility: float32 [18432, 18432], P('row', 'col'), as said below
Outputs:
- factored: float32 [18432, 18432], P('row', 'col')
Inputs may be any that keep to these rules, and one draw needn't show every extreme that they name: `mobility`: the matrix is exactly symmetric; its block at the global indices 0 to 767 is positive definite with all eigenvalues 1 or more; the rest is a random symmetric stand-in.
All inputs are finite; a program needn't handle non-finite values.
Results may differ from a plain program's by a relative error of at most 0.00005.
Values sent between devices are 32-bit elements; how exact they have to be, the bound alone decides.
A program may use at most 128 MiB of HBM per device.

v0:
```python
import functools

import jax
import jax.numpy as jnp
from jax import lax
from jax.experimental import pallas as pl
from jax.experimental.pallas import tpu as pltpu
from jax.sharding import PartitionSpec as P

B = 768
T = 128
NB = B // T
NX, NY = 4, 4
NZ = 8
R = NX * NY
C = NZ * 2
F = jnp.float32
BF = jnp.bfloat16
MESH = pl.DeviceIdType.MESH
HIGHEST = lax.Precision.HIGHEST


def dot(a, b):
    return lax.dot_general(a, b, (((1,), (0,)), ((), ())), precision=HIGHEST, preferred_element_type=F)


def dot_t(a, b):
    return lax.dot_general(a, b, (((0,), (0,)), ((), ())), precision=HIGHEST, preferred_element_type=F)


def factor_diag(d_ref, v_ref):
    sub = lax.broadcasted_iota(jnp.int32, (8, T), 0)
    lane = lax.broadcasted_iota(jnp.int32, (8, T), 1)

    def wide(x):
        return jnp.broadcast_to(x, (8, T))

    count = T // 8
    a = [d_ref[8 * q : 8 * q + 8, :] for q in range(count)]
    v = [jnp.where(lane == sub + 8 * q, 1.0, 0.0).astype(F) for q in range(count)]
    for p in range(count):
        c = [wide(a[p][:, 8 * p + i : 8 * p + i + 1]) for i in range(8)]
        wa, wv, fv, scale = a[p], v[p], v[p], None
        for i in range(8):
            pivot = wide(c[i][i : i + 1, :])
            inverse = 1.0 / pivot
            m = c[i] * inverse
            here = sub == i
            for k in range(i + 1, 8):
                row = wide(c[k][i : i + 1, :])
                c[k] = jnp.where(here, row * inverse, c[k] - m * row)
            if p < count - 1:
                row = wide(wa[i : i + 1, :])
                wa = jnp.where(here, row * inverse, wa - m * row)
                row = wide(wv[i : i + 1, :])
                wv = jnp.where(here, row * inverse, wv - m * row)
            row = wide(fv[i : i + 1, :])
            fv = fv - jnp.where(sub > i, m, 0.0) * row
            root = lax.rsqrt(pivot)
            scale = root if scale is None else jnp.where(here, root, scale)
        v_ref[8 * p : 8 * p + 8, :] = fv * scale
        if p == count - 1:
            break
        rows_a = [wide(wa[i : i + 1, :]) for i in range(8)]
        rows_v = [wide(wv[i : i + 1, :]) for i in range(8)]
        for q in range(p + 1, count):
            co = [wide(a[q][:, 8 * p + i : 8 * p + i + 1]) for i in range(8)]
            for i in range(8):
                a[q] = a[q] - co[i] * rows_a[i]
                v[q] = v[q] - co[i] * rows_v[i]


def remote(src, dst, send, recv, device):
    return pltpu.make_async_remote_copy(
        src_ref=src, dst_ref=dst, send_sem=send, recv_sem=recv, device_id=device, device_id_type=MESH
    )


def gather_kernel(
    mob, top, left, y_ref, sq, u_scr, d_scr, v_scr,
    as_, ar, bs, br, cs, cr, sts, str_, sls, slr, loc, t1s, t1r, t2s, t2r, us, ur, ds, dr, ws, wr,
):
    row, col = lax.axis_index("row"), lax.axis_index("col")
    x, y = row // NY, row % NY
    z, core = col // 2, col % 2
    other = z * 2 + 1 - core
    piece = mob.shape[0] // C

    barrier = pltpu.get_barrier_semaphore()

    @pl.loop(0, R)
    def _(i):
        @pl.when(i != row)
        def _():
            pl.semaphore_signal(barrier, inc=1, device_id=(i, col), device_id_type=MESH)

    @pl.loop(0, C)
    def _(i):
        @pl.when(i != col)
        def _():
            pl.semaphore_signal(barrier, inc=1, device_id=(row, i), device_id_type=MESH)

    pl.semaphore_wait(barrier, R + C - 2)

    def a_copy(to, slot, half):
        return remote(
            mob.at[0:T, 0:T], sq.at[half, pl.ds(row_at(row), T), pl.ds(pl.multiple_of(slot * T, T), T)],
            as_.at[to], ar.at[slot], (row, to * 2 + half),
        )

    def row_at(r):
        return pl.multiple_of(r * T, T)

    a_sender = jnp.logical_and(row < NB, jnp.logical_and(col < NB, col >= row))

    def a_local():
        slot = col // 2
        return pltpu.make_async_copy(
            mob.at[0:T, 0:T],
            sq.at[core, pl.ds(row_at(row), T), pl.ds(pl.multiple_of(slot * T, T), T)], ar.at[slot],
        )

    @pl.when(a_sender)
    def _():
        a_local().start()

        @pl.loop(0, NZ)
        def _(to):
            @pl.when(to != z)
            def _():
                a_copy(to, col // 2, core).start()

    def top_piece(i):
        return remote(
            mob.at[pl.ds(pl.multiple_of(i * 8, 8), 8), :], top.at[row, i // NY, i % NY], sts.at[i], str_.at[row], (i, col)
        )

    def top_own():
        return pltpu.make_async_copy(
            mob.at[pl.ds(pl.multiple_of(row * 8, 8), 8), :], top.at[row, x, y], loc.at[0]
        )

    def left_piece(i):
        return remote(
            mob.at[pl.ds(pl.multiple_of(i * piece, 8), piece), 0:T],
            left.at[i, :, pl.ds(pl.multiple_of(col * T, T), T)], sls.at[i], slr.at[col], (row, i),
        )

    def left_own():
        return pltpu.make_async_copy(
            mob.at[pl.ds(pl.multiple_of(col * piece, 8), piece), 0:T],
            left.at[col, :, pl.ds(pl.multiple_of(col * T, T), T)], loc.at[1],
        )

    def b_copy(r, slot, to):
        ref = sq.at[core, pl.ds(r * T, T), pl.ds(slot * T, T)]
        return remote(ref, ref, bs.at[slot, to], br.at[r, slot], (to, col))

    def c_copy(half, r, slot):
        ref = sq.at[half, pl.ds(r * T, T), pl.ds(slot * T, T)]
        return remote(ref, ref, cs.at[r, slot], cr.at[r, slot], (row, other))

    for r in range(NB):
        @pl.when(row == r)
        def _():
            for slot in range(NB // 2):
                @pl.when(2 * slot + core >= r)
                def _():
                    a_copy(z, slot, core).wait_recv()

                    @pl.loop(0, R)
                    def _(to):
                        @pl.when(to != row)
                        def _():
                            b_copy(r, slot, to).start()

    @pl.when(row < NB)
    def _():
        top_own().start()

        @pl.loop(0, R)
        def _(i):
            @pl.when(i != row)
            def _():
                top_piece(i).start()

    @pl.when(col < NB)
    def _():
        left_own().start()

        @pl.loop(0, C)
        def _(i):
            @pl.when(i != col)
            def _():
                left_piece(i).start()

    def swap_strip(r):
        for slot in range(NB // 2):
            @pl.when(2 * slot + core >= r)
            def _():
                @pl.when(row != r)
                def _():
                    b_copy(r, slot, row).wait_recv()

                c_copy(core, r, slot).start()

    def wait_strip(r):
        for slot in range(NB // 2):
            @pl.when(2 * slot + 1 - core >= r)
            def _():
                c_copy(1 - core, r, slot).wait_recv()

    def wait_scatter():
        for g in range(NB):
            @pl.when(row != g)
            def _():
                remote(top.at[g, x, y], top.at[g, x, y], sts.at[0], str_.at[g], (row, col)).wait_recv()

            @pl.when(col != g)
            def _():
                ref = left.at[col, :, pl.ds(g * T, T)]
                remote(ref, ref, sls.at[0], slr.at[g], (row, col)).wait_recv()

        @pl.when(row < NB)
        def _():
            top_own().wait()

        @pl.when(col < NB)
        def _():
            left_own().wait()

    H = NB // 2

    def t1(axis, src, to):
        if axis == 0:
            ref, dev = top.at[0:H, src, y], (to * NY + y, col)
        else:
            ref, dev = top.at[H:NB, x, src], (x * NY + to, col)
        return remote(ref, ref, t1s.at[axis, to], t1r.at[axis, src], dev)

    def t2(axis, src, to):
        if axis == 0:
            ref, dev = top.at[0:H, :, src], (x * NY + to, col)
        else:
            ref, dev = top.at[H:NB, src], (to * NY + y, col)
        return remote(ref, ref, t2s.at[axis, to], t2r.at[axis, src], dev)

    def spread(make, mine):
        for axis in range(2):
            for to in range(4):
                @pl.when(to != mine[axis])
                def _():
                    make(axis, mine[axis], to).start()

    def collect(make, mine, send):
        for axis in range(2):
            for to in range(4):
                @pl.when(to != mine[axis])
                def _():
                    if send:
                        make(axis, mine[axis], to).wait_send()
                    else:
                        make(axis, to, mine[axis]).wait_recv()

    def up(step, at):
        ref = left.at[(at - step + NZ) % NZ * 2 + core]
        return remote(ref, ref, us.at[step], ur.at[step], (row, (z + 1) % NZ * 2 + core))

    def down(step, at):
        ref = left.at[(at + step) % NZ * 2 + core]
        return remote(ref, ref, ds.at[step], dr.at[step], (row, (z + NZ - 1) % NZ * 2 + core))

    UP, DOWN = 4, 3

    def swap(which, half, zz):
        ref = left.at[zz * 2 + half]
        return remote(ref, ref, ws.at[which], wr.at[which], (row, other))

    def set_of(which):
        if which <= UP:
            return (z - which + NZ) % NZ
        return (z + which - UP) % NZ

    def hop(step):
        if step > 0:
            up(step - 1, (z - 1 + NZ) % NZ).wait_recv()
            swap(step, core, set_of(step)).start()
            if step - 1 < DOWN:
                down(step - 1, (z + 1) % NZ).wait_recv()
                swap(UP + step, core, set_of(UP + step)).start()
        else:
            swap(0, core, z).start()
        if step < UP:
            up(step, z).start()
        if step < DOWN:
            down(step, z).start()

    y_ref[...] = jnp.zeros_like(y_ref)
    swap_strip(0)

    def tile(r, c):
        return sq.at[c % 2, pl.ds(r * T, T), pl.ds(c // 2 * T, T)]

    @pl.loop(0, NB)
    def _(k):
        for kk in range(NB):
            lo, hi = kk * T, kk * T + T

            @pl.when(k == kk)
            def _():
                wait_strip(kk)
                if kk == 0:
                    d_scr[...] = tile(0, 0)[...]
                else:
                    w = u_scr[:lo, lo:hi]
                    d_scr[...] = tile(kk, kk)[...] - dot_t(w, u_scr[:lo, lo:hi])
                if kk + 1 < NB:
                    swap_strip(kk + 1)
                if kk == 0:
                    wait_scatter()
                    spread(t1, (x, y))
                if kk == 1:
                    collect(t1, (x, y), False)
                    spread(t2, (y, x))
                if kk <= UP:
                    hop(kk)

        factor_diag(d_scr, v_scr)
        for kk in range(NB):
            lo, hi = kk * T, kk * T + T

            @pl.when(k == kk)
            def _():
                inverse = v_scr[...]
                y_ref[lo:hi, lo:hi] = inverse
                if kk > 0:
                    w = u_scr[:lo, lo:hi]
                    y_ref[lo:hi, :lo] = -dot(inverse, dot_t(w, y_ref[:lo, :lo]))
                if hi < B:
                    r = jnp.concatenate([tile(kk, c)[...] for c in range(kk + 1, NB)], axis=1)
                    if kk > 0:
                        r = r - dot_t(w, u_scr[:lo, hi:])
                    u_scr[lo:hi, hi:] = dot(inverse, r)

    collect(t2, (y, x), False)
    for which in range(NZ):
        swap(which, 1 - core, set_of(which)).wait_recv()

    @pl.when(a_sender)
    def _():
        @pl.loop(0, NZ)
        def _(to):
            @pl.when(to != z)
            def _():
                a_copy(to, col // 2, core).wait_send()

    for r in range(NB):
        @pl.when(row == r)
        def _():
            for slot in range(NB // 2):
                @pl.when(2 * slot + core >= r)
                def _():
                    @pl.loop(0, R)
                    def _(to):
                        @pl.when(to != row)
                        def _():
                            b_copy(r, slot, to).wait_send()

        for slot in range(NB // 2):
            @pl.when(2 * slot + core >= r)
            def _():
                c_copy(core, r, slot).wait_send()

    @pl.when(row < NB)
    def _():
        @pl.loop(0, R)
        def _(i):
            @pl.when(i != row)
            def _():
                top_piece(i).wait_send()

    @pl.when(col < NB)
    def _():
        @pl.loop(0, C)
        def _(i):
            @pl.when(i != col)
            def _():
                left_piece(i).wait_send()

    collect(t1, (x, y), True)
    collect(t2, (y, x), True)
    for step in range(UP):
        up(step, z).wait_send()
    for step in range(DOWN):
        down(step, z).wait_send()
    for which in range(NZ):
        swap(which, core, set_of(which)).wait_send()


def gather(mobility):
    rows, cols = mobility.shape
    D = pltpu.SemaphoreType.DMA
    top, left, inverse = pl.pallas_call(
        gather_kernel,
        out_shape=(
            jax.ShapeDtypeStruct((NB, NX, NY, T // R, cols), F),
            jax.ShapeDtypeStruct((C, rows // C, B), F),
            jax.ShapeDtypeStruct((B, B), F),
        ),
        in_specs=[pl.BlockSpec(memory_space=pl.ANY)],
        out_specs=(
            pl.BlockSpec(memory_space=pl.ANY),
            pl.BlockSpec(memory_space=pl.ANY),
            pl.BlockSpec(memory_space=pltpu.VMEM),
        ),
        scratch_shapes=[
            pltpu.VMEM((2, B, B // 2), F),
            pltpu.VMEM((B, B), F),
            pltpu.VMEM((T, T), F),
            pltpu.VMEM((T, T), F),
            D((NZ,)), D((NB // 2,)),
            D((NB // 2, R)), D((NB, NB // 2)),
            D((NB, NB // 2)), D((NB, NB // 2)),
            D((R,)), D((NB,)), D((C,)), D((NB,)), D((2,)),
            D((2, 4)), D((2, 4)), D((2, 4)), D((2, 4)),
            D((4,)), D((4,)), D((3,)), D((3,)), D((NZ,)), D((NZ,)),
        ],
        compiler_params=pltpu.CompilerParams(
            collective_id=0, has_side_effects=True, vmem_limit_bytes=32 << 20
        ),
    )(mobility)
    return top.reshape(B, cols), left.reshape(rows, B), inverse


def halves(x):
    high = x.astype(BF)
    return high, (x - high.astype(F)).astype(BF)


def update_kernel(steps, mob, left, top, inv, out, i3, t3, xl):
    m = pl.program_id(0)
    BLK = 256

    @pl.when(m == 0)
    def _():
        high, low = halves(inv[...])
        i3[0] = high
        i3[1] = low
        for b in range(B // BLK):
            high, low = halves(top[b * BLK : (b + 1) * BLK, :])
            t3[b * BLK : (b + 1) * BLK, :] = high
            t3[B + b * BLK : B + (b + 1) * BLK, :] = low
        for b in reversed(range(B // BLK)):
            lo, hi = b * BLK, (b + 1) * BLK
            ih, il = i3[0, lo:hi, :hi], i3[1, lo:hi, :hi]
            th, tl = t3[:hi, :], t3[B : B + hi, :]
            s = jnp.dot(ih, th, preferred_element_type=F)
            s += jnp.dot(ih, tl, preferred_element_type=F)
            s += jnp.dot(il, th, preferred_element_type=F)
            high, low = halves(s)
            t3[lo:hi, :] = high
            t3[B + lo : B + hi, :] = low

    lh, ll = halves(left[...])
    dims = (((1,), (1,)), ((), ()))
    for b in range(B // BLK):
        lo, hi = b * BLK, (b + 1) * BLK
        ih, il = i3[0, lo:hi, :hi], i3[1, lo:hi, :hi]
        s = lax.dot_general(lh[:, :hi], ih, dims, preferred_element_type=F)
        s += lax.dot_general(lh[:, :hi], il, dims, preferred_element_type=F)
        s += lax.dot_general(ll[:, :hi], ih, dims, preferred_element_type=F)
        xl[:, lo:hi] = s
    xh, xo = halves(xl[...])
    th, tl = t3[:B, :], t3[B:, :]
    s = jnp.dot(xh, th, preferred_element_type=F)
    s += jnp.dot(xh, tl, preferred_element_type=F)
    s += jnp.dot(xo, th, preferred_element_type=F)
    out[...] = mob[...] - s
    col = lax.axis_index("col")

    @pl.when(col < NB)
    def _():
        out[:, 0:T] = xl[:, pl.ds(pl.multiple_of(jnp.minimum(col, NB - 1) * T, T), T)]


def update(mobility, left, top, inverse):
    rows, cols = mobility.shape
    steps = 6
    tm = rows // steps
    return pl.pallas_call(
        functools.partial(update_kernel, steps),
        grid=(steps,),
        out_shape=jax.ShapeDtypeStruct(mobility.shape, F),
        in_specs=[
            pl.BlockSpec((tm, cols), lambda i: (i, 0)),
            pl.BlockSpec((tm, B), lambda i: (i, 0)),
            pl.BlockSpec((B, cols), lambda i: (0, 0)),
            pl.BlockSpec((B, B), lambda i: (0, 0)),
        ],
        out_specs=pl.BlockSpec((tm, cols), lambda i: (i, 0)),
        scratch_shapes=[
            pltpu.VMEM((2, B, B), BF),
            pltpu.VMEM((2 * B, cols), BF),
            pltpu.VMEM((tm, B), F),
        ],
        compiler_params=pltpu.CompilerParams(vmem_limit_bytes=48 << 20),
    )(mobility, left, top, inverse)


def on_device(mobility):
    top, left, inverse = gather(mobility)
    return update(mobility, left, top, inverse)


def solution(mesh):
    return jax.shard_map(
        on_device,
        mesh=mesh,
        in_specs=(P("row", "col"),),
        out_specs=P("row", "col"),
        check_vma=False,
    )
```

profile of v0, /device:TPU:4, one launch (start us, length us, event | category | flops | bytes accessed | tf_op | source)
XLA Modules:
  0.0 134.3 jit_solution(8844866874145915027)
XLA Ops:
  0.0 0.0 copy-start
  0.0 2.5 %copy-done = f32[1152,1152]{1,0:T(8,128)S(1)} copy-done((f32[1152,1152]{1,0:T(8,128)S(1)}, f32[1152,1152]{1,0:T(8,128)}, u32[]{:S(2)}) %copy-start) | copy-done | bytes 5308440
  2.5 107.4 %shard_map.17 = (f32[6,4,4,8,1152]{4,3,2,1,0:T(8,128)S(1)}, f32[16,72,768]{2,1,0:T(8,128)S(1)}, f32[768,768]{1,0:T(8,128)S(1)}) custom-call(f32[1152,1152]{1,0:T(8,128)S(1)} %copy-done), custom_call_target="tpu_custom_call" | custom-call | tf_op jit(solution)/shard_map/pallas_call | solution.py:403
  109.9 0.0 copy-start.1
  109.9 1.7 %copy-done.1 = f32[6,4,4,8,1152]{4,3,2,1,0:T(8,128)} copy-done((f32[6,4,4,8,1152]{4,3,2,1,0:T(8,128)}, f32[6,4,4,8,1152]{4,3,2,1,0:T(8,128)S(1)}, u32[]{:S(2)}) %copy-start.1) | copy-done | bytes 3538968
  111.6 22.6 %shard_map.18 = f32[1152,1152]{1,0:T(8,128)} custom-call(f32[1152,1152]{1,0:T(8,128)} %mob.3, f32[1152,768]{1,0:T(8,128)S(1)} %bitcast.3, f32[768,1152]{1,0:T(8,128)} %bitcast.2, f32[768,768]{1,0:T(8,128)S(1)} %get-tuple-element.10.inv), custom_call_target="tpu_custom_call" | custom-call | tf_op jit(solution)/shard_map/pallas_call | solution.py:490
Async XLA Ops:
  0.0 2.5 %copy-start = (f32[1152,1152]{1,0:T(8,128)S(1)}, f32[1152,1152]{1,0:T(8,128)}, u32[]{:S(2)}) copy-start(f32[1152,1152]{1,0:T(8,128)} %mob.3) | copy-start | bytes 15925252
  109.9 1.7 %copy-start.1 = (f32[6,4,4,8,1152]{4,3,2,1,0:T(8,128)}, f32[6,4,4,8,1152]{4,3,2,1,0:T(8,128)S(1)}, u32[]{:S(2)}) copy-start(f32[6,4,4,8,1152]{4,3,2,1,0:T(8,128)S(1)} %get-tuple-element.9) | copy-start | bytes 10616836
where the time goes:
time: 134 us
  Pallas kernels  130 us (97%)
  local copies, waits for them, and re-layouts  4.24 us (3%)
    pallas_call x1, Pallas kernels, gather(): pl.pallas_call(gather_kernel, out_shape=(jax.ShapeDtypeStruct((NB, NX, NY...  107 us
    pallas_call x1, Pallas kernels, update(): pl.pallas_call(functools.partial(update_kernel, steps), grid=(steps,), ou...  22.6 us
    unnamed x4, local copies, waits for them, and re-layouts  4.24 us

commit v1 on v0

--- a/solution.py
+++ b/solution.py
@@ -28,46 +28,78 @@
     return lax.dot_general(a, b, (((0,), (0,)), ((), ())), precision=HIGHEST, preferred_element_type=F)
 
 
-def factor_diag(d_ref, v_ref):
+def factor_diag(d_ref, v_ref, between):
     sub = lax.broadcasted_iota(jnp.int32, (8, T), 0)
-    lane = lax.broadcasted_iota(jnp.int32, (8, T), 1)
 
     def wide(x):
         return jnp.broadcast_to(x, (8, T))
 
-    count = T // 8
-    a = [d_ref[8 * q : 8 * q + 8, :] for q in range(count)]
-    v = [jnp.where(lane == sub + 8 * q, 1.0, 0.0).astype(F) for q in range(count)]
-    for p in range(count):
-        c = [wide(a[p][:, 8 * p + i : 8 * p + i + 1]) for i in range(8)]
-        wa, wv, fv, scale = a[p], v[p], v[p], None
-        for i in range(8):
-            pivot = wide(c[i][i : i + 1, :])
-            inverse = 1.0 / pivot
-            m = c[i] * inverse
-            here = sub == i
-            for k in range(i + 1, 8):
-                row = wide(c[k][i : i + 1, :])
-                c[k] = jnp.where(here, row * inverse, c[k] - m * row)
-            if p < count - 1:
-                row = wide(wa[i : i + 1, :])
-                wa = jnp.where(here, row * inverse, wa - m * row)
-                row = wide(wv[i : i + 1, :])
-                wv = jnp.where(here, row * inverse, wv - m * row)
-            row = wide(fv[i : i + 1, :])
-            fv = fv - jnp.where(sub > i, m, 0.0) * row
-            root = lax.rsqrt(pivot)
-            scale = root if scale is None else jnp.where(here, root, scale)
-        v_ref[8 * p : 8 * p + 8, :] = fv * scale
-        if p == count - 1:
-            break
-        rows_a = [wide(wa[i : i + 1, :]) for i in range(8)]
-        rows_v = [wide(wv[i : i + 1, :]) for i in range(8)]
-        for q in range(p + 1, count):
-            co = [wide(a[q][:, 8 * p + i : 8 * p + i + 1]) for i in range(8)]
+    count, group = T // 8, T // 16
+    eye = lax.broadcasted_iota(jnp.int32, (T, T), 0) == lax.broadcasted_iota(jnp.int32, (T, T), 1)
+    v_ref[...] = jnp.where(eye, 1.0, 0.0).astype(F)
+    for first in range(0, count, group):
+        end = first + group
+        last = end == count
+        a = {q: d_ref[8 * q : 8 * q + 8, :] for q in range(first, end)}
+        v = {q: v_ref[8 * q : 8 * q + 8, :] for q in range(first, end)}
+        done_a, done_v, ahead = [], [], None
+        for p in range(first, end):
+            c = ahead
+            if c is None:
+                c = [wide(a[p][:, 8 * p + i : 8 * p + i + 1]) for i in range(8)]
+            near, far = p + 1 < end, p + 2 < end
+            if near:
+                co = [wide(a[p + 1][:, 8 * p + i : 8 * p + i + 1]) for i in range(8)]
+                ahead = [wide(a[p + 1][:, 8 * p + 8 + k : 8 * p + 9 + k]) for k in range(8)]
+            wa = fa = a[p]
+            wv = fv = v[p]
+            scale = inverses = None
             for i in range(8):
-                a[q] = a[q] - co[i] * rows_a[i]
-                v[q] = v[q] - co[i] * rows_v[i]
+                here = sub == i
+                pivot = wide(c[i][i : i + 1, :])
+                inverse = 1.0 / pivot
+                m = jnp.where(here, 0.0, c[i]) * inverse
+                below = jnp.where(sub > i, c[i], 0.0) * inverse
+                for k in range(i + 1, 8):
+                    c[k] = c[k] - m * wide(c[k][i : i + 1, :])
+                row_a, row_v = wide(fa[i : i + 1, :]), wide(fv[i : i + 1, :])
+                if near:
+                    t = co[i] * inverse
+                    for k in range(8):
+                        ahead[k] = ahead[k] - t * wide(co[i][k : k + 1, :])
+                    a[p + 1] = a[p + 1] - t * row_a
+                    v[p + 1] = v[p + 1] - t * row_v
+                    for k in range(i + 1, 8):
+                        co[k] = co[k] - co[i] * wide(m[k : k + 1, :])
+                if far:
+                    wa = wa - m * wide(wa[i : i + 1, :])
+                    wv = wv - m * wide(wv[i : i + 1, :])
+                fv = fv - below * row_v
+                fa = fa - below * row_a
+                root = lax.rsqrt(pivot)
+                scale = root if scale is None else jnp.where(here, root, scale)
+                inverses = inverse if inverses is None else jnp.where(here, inverse, inverses)
+            fv = fv * scale
+            v_ref[8 * p : 8 * p + 8, :] = fv
+            if not last:
+                done_a.append(fa * scale)
+                done_v.append(fv)
+            if not far:
+                continue
+            wa, wv = wa * inverses, wv * inverses
+            rows_a = [wide(wa[i : i + 1, :]) for i in range(8)]
+            rows_v = [wide(wv[i : i + 1, :]) for i in range(8)]
+            for q in range(p + 2, end):
+                cq = [wide(a[q][:, 8 * p + i : 8 * p + i + 1]) for i in range(8)]
+                for i in range(8):
+                    a[q] = a[q] - cq[i] * rows_a[i]
+                    v[q] = v[q] - cq[i] * rows_v[i]
+        if not last:
+            u, w = jnp.concatenate(done_a, axis=0), jnp.concatenate(done_v, axis=0)
+            r = dot_t(u, jnp.concatenate([u, w], axis=1))
+            d_ref[8 * end :, :] -= r[8 * end :, :T]
+            v_ref[8 * end :, :] -= r[8 * end :, T:]
+            between()
 
 
 def remote(src, dst, send, recv, device):
@@ -78,7 +110,7 @@
 
 def gather_kernel(
     mob, top, left, y_ref, sq, u_scr, d_scr, v_scr,
-    as_, ar, bs, br, cs, cr, sts, str_, sls, slr, loc, t1s, t1r, t2s, t2r, us, ur, ds, dr, ws, wr,
+    as_, ar, b1s, b2s, br, cs, cr, sts, str_, sls, slr, loc, ts, tr, us, ur, ds, dr, ws, wr,
 ):
     row, col = lax.axis_index("row"), lax.axis_index("col")
     x, y = row // NY, row % NY
@@ -152,9 +184,33 @@
             left.at[col, :, pl.ds(pl.multiple_of(col * T, T), T)], loc.at[1],
         )
 
-    def b_copy(r, slot, to):
+    @pl.when(row < NB)
+    def _():
+        top_own().start()
+
+        @pl.loop(0, R)
+        def _(i):
+            @pl.when(i != row)
+            def _():
+                top_piece(i).start()
+
+    @pl.when(col < NB)
+    def _():
+        left_own().start()
+
+        @pl.loop(0, C)
+        def _(i):
+            @pl.when(i != col)
+            def _():
+                left_piece(i).start()
+
+    def b1(r, slot, to):
         ref = sq.at[core, pl.ds(r * T, T), pl.ds(slot * T, T)]
-        return remote(ref, ref, bs.at[slot, to], br.at[r, slot], (to, col))
+        return remote(ref, ref, b1s.at[slot, to], br.at[r, slot], (to * NY + y, col))
+
+    def b2(r, slot, to):
+        ref = sq.at[core, pl.ds(r * T, T), pl.ds(slot * T, T)]
+        return remote(ref, ref, b2s.at[r, slot, to], br.at[r, slot], (x * NY + to, col))
 
     def c_copy(half, r, slot):
         ref = sq.at[half, pl.ds(r * T, T), pl.ds(slot * T, T)]
@@ -168,39 +224,38 @@
                 def _():
                     a_copy(z, slot, core).wait_recv()
 
-                    @pl.loop(0, R)
+                    @pl.loop(0, NX)
                     def _(to):
-                        @pl.when(to != row)
+                        @pl.when(to != x)
                         def _():
-                            b_copy(r, slot, to).start()
-
-    @pl.when(row < NB)
-    def _():
-        top_own().start()
-
-        @pl.loop(0, R)
-        def _(i):
-            @pl.when(i != row)
-            def _():
-                top_piece(i).start()
-
-    @pl.when(col < NB)
-    def _():
-        left_own().start()
-
-        @pl.loop(0, C)
-        def _(i):
-            @pl.when(i != col)
-            def _():
-                left_piece(i).start()
+                            b1(r, slot, to).start()
+
+    def forward(r):
+        @pl.when(y == r % NY)
+        def _():
+            for slot in range(NB // 2):
+                @pl.when(2 * slot + core >= r)
+                def _():
+                    @pl.when(x != r // NY)
+                    def _():
+                        b1(r, slot, x).wait_recv()
+
+                    @pl.loop(0, NY)
+                    def _(to):
+                        @pl.when(to != y)
+                        def _():
+                            b2(r, slot, to).start()
+
+    for r in range(NY):
+        forward(r)
 
     def swap_strip(r):
         for slot in range(NB // 2):
             @pl.when(2 * slot + core >= r)
             def _():
-                @pl.when(row != r)
+                @pl.when(y != r % NY)
                 def _():
-                    b_copy(r, slot, row).wait_recv()
+                    b2(r, slot, y).wait_recv()
 
                 c_copy(core, r, slot).start()
 
@@ -210,57 +265,63 @@
             def _():
                 c_copy(1 - core, r, slot).wait_recv()
 
-    def wait_scatter():
+    def wait_top():
         for g in range(NB):
             @pl.when(row != g)
             def _():
-                remote(top.at[g, x, y], top.at[g, x, y], sts.at[0], str_.at[g], (row, col)).wait_recv()
-
+                ref = top.at[g, x, y]
+                remote(ref, ref, sts.at[0], str_.at[g], (row, col)).wait_recv()
+
+        @pl.when(row < NB)
+        def _():
+            top_own().wait()
+
+    def wait_left():
+        for g in range(NB):
             @pl.when(col != g)
             def _():
                 ref = left.at[col, :, pl.ds(g * T, T)]
                 remote(ref, ref, sls.at[0], slr.at[g], (row, col)).wait_recv()
 
-        @pl.when(row < NB)
-        def _():
-            top_own().wait()
-
         @pl.when(col < NB)
         def _():
             left_own().wait()
 
     H = NB // 2
-
-    def t1(axis, src, to):
-        if axis == 0:
-            ref, dev = top.at[0:H, src, y], (to * NY + y, col)
+    PART = 640
+
+    def tcopy(phase, axis, kind, at):
+        src = (at + (0, 0, 3, 1)[kind]) % 4
+        to = (at + (1, 3, 1, 3)[kind]) % 4
+        if phase == 0:
+            lanes = (slice(None), slice(None), slice(0, PART), slice(PART, None))[kind]
+            ref = top.at[0:H, src, y, :, lanes] if axis == 0 else top.at[H:NB, x, src, :, lanes]
         else:
-            ref, dev = top.at[H:NB, x, src], (x * NY + to, col)
-        return remote(ref, ref, t1s.at[axis, to], t1r.at[axis, src], dev)
-
-    def t2(axis, src, to):
-        if axis == 0:
-            ref, dev = top.at[0:H, :, src], (x * NY + to, col)
-        else:
-            ref, dev = top.at[H:NB, src], (to * NY + y, col)
-        return remote(ref, ref, t2s.at[axis, to], t2r.at[axis, src], dev)
-
-    def spread(make, mine):
+            part = (slice(None), slice(None), slice(0, 2), slice(2, 4))[kind]
+            ref = top.at[0:H, part, src] if axis == 1 else top.at[H:NB, src, part]
+        device = (to * NY + y, col) if axis == 0 else (x * NY + to, col)
+        return remote(ref, ref, ts.at[phase, axis, kind], tr.at[phase, axis, kind], device)
+
+    place = (x, y)
+
+    def spread(phase, step):
         for axis in range(2):
-            for to in range(4):
-                @pl.when(to != mine[axis])
-                def _():
-                    make(axis, mine[axis], to).start()
-
-    def collect(make, mine, send):
+            if step == 1:
+                for kind in range(2):
+                    tcopy(phase, axis, kind, (place[axis] + (3, 1)[kind]) % 4).wait_recv()
+            for kind in range(2 * step, 2 * step + 2):
+                tcopy(phase, axis, kind, place[axis]).start()
+
+    def spread_end(phase):
         for axis in range(2):
-            for to in range(4):
-                @pl.when(to != mine[axis])
-                def _():
-                    if send:
-                        make(axis, mine[axis], to).wait_send()
-                    else:
-                        make(axis, to, mine[axis]).wait_recv()
+            for kind in range(2, 4):
+                tcopy(phase, axis, kind, (place[axis] + (0, 0, 3, 1)[kind]) % 4).wait_recv()
+
+    def spread_sent():
+        for phase in range(2):
+            for axis in range(2):
+                for kind in range(4):
+                    tcopy(phase, axis, kind, place[axis]).wait_send()
 
     def up(step, at):
         ref = left.at[(at - step + NZ) % NZ * 2 + core]
@@ -317,15 +378,28 @@
                 if kk + 1 < NB:
                     swap_strip(kk + 1)
                 if kk == 0:
-                    wait_scatter()
-                    spread(t1, (x, y))
-                if kk == 1:
-                    collect(t1, (x, y), False)
-                    spread(t2, (y, x))
-                if kk <= UP:
-                    hop(kk)
-
-        factor_diag(d_scr, v_scr)
+                    forward(4)
+                    forward(5)
+                if kk == 2:
+                    spread_end(0)
+                    spread(1, 0)
+                if kk == 4:
+                    spread(1, 1)
+
+        def between():
+            for kk in range(NB):
+                @pl.when(k == kk)
+                def _():
+                    if kk == 0:
+                        wait_top()
+                        spread(0, 0)
+                    if kk == 1:
+                        spread(0, 1)
+                        wait_left()
+                    if kk > 0:
+                        hop(kk - 1)
+
+        factor_diag(d_scr, v_scr, between)
         for kk in range(NB):
             lo, hi = kk * T, kk * T + T
 
@@ -342,7 +416,7 @@
                         r = r - dot_t(w, u_scr[:lo, hi:])
                     u_scr[lo:hi, hi:] = dot(inverse, r)
 
-    collect(t2, (y, x), False)
+    spread_end(1)
     for which in range(NZ):
         swap(which, 1 - core, set_of(which)).wait_recv()
 
@@ -360,11 +434,22 @@
             for slot in range(NB // 2):
                 @pl.when(2 * slot + core >= r)
                 def _():
-                    @pl.loop(0, R)
+                    @pl.loop(0, NX)
                     def _(to):
-                        @pl.when(to != row)
+                        @pl.when(to != x)
                         def _():
-                            b_copy(r, slot, to).wait_send()
+                            b1(r, slot, to).wait_send()
+
+        @pl.when(y == r % NY)
+        def _():
+            for slot in range(NB // 2):
+                @pl.when(2 * slot + core >= r)
+                def _():
+                    @pl.loop(0, NY)
+                    def _(to):
+                        @pl.when(to != y)
+                        def _():
+                            b2(r, slot, to).wait_send()
 
         for slot in range(NB // 2):
             @pl.when(2 * slot + core >= r)
@@ -387,8 +472,7 @@
             def _():
                 left_piece(i).wait_send()
 
-    collect(t1, (x, y), True)
-    collect(t2, (y, x), True)
+    spread_sent()
     for step in range(UP):
         up(step, z).wait_send()
     for step in range(DOWN):
@@ -419,10 +503,10 @@
             pltpu.VMEM((T, T), F),
             pltpu.VMEM((T, T), F),
             D((NZ,)), D((NB // 2,)),
-            D((NB // 2, R)), D((NB, NB // 2)),
+            D((NB // 2, NX)), D((NB, NB // 2, NY)), D((NB, NB // 2)),
             D((NB, NB // 2)), D((NB, NB // 2)),
             D((R,)), D((NB,)), D((C,)), D((NB,)), D((2,)),
-            D((2, 4)), D((2, 4)), D((2, 4)), D((2, 4)),
+            D((2, 2, 4)), D((2, 2, 4)),
             D((4,)), D((4,)), D((3,)), D((3,)), D((NZ,)), D((NZ,)),
         ],
         compiler_params=pltpu.CompilerParams(

time: 134 us -> 104 us (0.78)
  the two profiles are of different devices: /device:TPU:4 before, /device:TPU:1 now
where the time goes in v1:
time: 104 us; the launch traced here: 102 us
  Pallas kernels  97.8 us (94%)
  local copies, waits for them, and re-layouts  4.24 us (4%)
    pallas_call x1, Pallas kernels, gather(): pl.pallas_call(gather_kernel, out_shape=(jax.ShapeDtypeStruct((NB, NX, NY...  75.1 us
    pallas_call x1, Pallas kernels, update(): pl.pallas_call(functools.partial(update_kernel, steps), grid=(steps,), ou...  22.6 us
    unnamed x4, local copies, waits for them, and re-layouts  4.24 us

profile of v1, /device:TPU:1, one launch (start us, length us, event | category | flops | bytes accessed | tf_op | source)
XLA Modules:
  0.0 102.0 jit_solution(6567399264931640283)
XLA Ops:
  0.0 0.0 copy-start
  0.0 2.5 %copy-done = f32[1152,1152]{1,0:T(8,128)S(1)} copy-done((f32[1152,1152]{1,0:T(8,128)S(1)}, f32[1152,1152]{1,0:T(8,128)}, u32[]{:S(2)}) %copy-start) | copy-done | bytes 5308440
  2.5 75.1 %shard_map.17 = (f32[6,4,4,8,1152]{4,3,2,1,0:T(8,128)S(1)}, f32[16,72,768]{2,1,0:T(8,128)S(1)}, f32[768,768]{1,0:T(8,128)S(1)}) custom-call(f32[1152,1152]{1,0:T(8,128)S(1)} %copy-done), custom_call_target="tpu_custom_call" | custom-call | tf_op jit(solution)/shard_map/pallas_call | solution.py:487
  77.7 0.0 copy-start.1
  77.7 1.7 %copy-done.1 = f32[6,4,4,8,1152]{4,3,2,1,0:T(8,128)} copy-done((f32[6,4,4,8,1152]{4,3,2,1,0:T(8,128)}, f32[6,4,4,8,1152]{4,3,2,1,0:T(8,128)S(1)}, u32[]{:S(2)}) %copy-start.1) | copy-done | bytes 3538968
  79.4 22.6 %shard_map.18 = f32[1152,1152]{1,0:T(8,128)} custom-call(f32[1152,1152]{1,0:T(8,128)} %mob.3, f32[1152,768]{1,0:T(8,128)S(1)} %bitcast.3, f32[768,1152]{1,0:T(8,128)} %bitcast.2, f32[768,768]{1,0:T(8,128)S(1)} %get-tuple-element.10.inv), custom_call_target="tpu_custom_call" | custom-call | tf_op jit(solution)/shard_map/pallas_call | solution.py:574
Async XLA Ops:
  0.0 2.5 %copy-start = (f32[1152,1152]{1,0:T(8,128)S(1)}, f32[1152,1152]{1,0:T(8,128)}, u32[]{:S(2)}) copy-start(f32[1152,1152]{1,0:T(8,128)} %mob.3) | copy-start | bytes 15925252
  77.7 1.7 %copy-start.1 = (f32[6,4,4,8,1152]{4,3,2,1,0:T(8,128)}, f32[6,4,4,8,1152]{4,3,2,1,0:T(8,128)S(1)}, u32[]{:S(2)}) copy-start(f32[6,4,4,8,1152]{4,3,2,1,0:T(8,128)S(1)} %get-tuple-element.9) | copy-start | bytes 10616836

commit v2 on v1

--- a/solution.py
+++ b/solution.py
@@ -1,5 +1,3 @@
-import functools
-
 import jax
 import jax.numpy as jnp
 from jax import lax
@@ -10,6 +8,8 @@
 B = 768
 T = 128
 NB = B // T
+BLK = 256
+STEPS = 3
 NX, NY = 4, 4
 NZ = 8
 R = NX * NY
@@ -108,9 +108,14 @@
     )
 
 
-def gather_kernel(
-    mob, top, left, y_ref, sq, u_scr, d_scr, v_scr,
-    as_, ar, b1s, b2s, br, cs, cr, sts, str_, sls, slr, loc, ts, tr, us, ur, ds, dr, ws, wr,
+def halves(x):
+    high = x.astype(BF)
+    return high, (x - high.astype(F)).astype(BF)
+
+
+def panel_kernel(
+    mob, out, top, left, y_ref, sq, u_scr, d_scr, v_scr, buf, i3, t3, xl,
+    as_, ar, b1s, b2s, br, cs, cr, sts, str_, sls, slr, loc, ts, tr, us, ur, ds, dr, ws, wr, os_,
 ):
     row, col = lax.axis_index("row"), lax.axis_index("col")
     x, y = row // NY, row % NY
@@ -248,6 +253,8 @@
 
     for r in range(NY):
         forward(r)
+
+    pltpu.make_async_copy(mob, buf, loc.at[2]).start()
 
     def swap_strip(r):
         for slot in range(NB // 2):
@@ -381,10 +388,11 @@
                     forward(4)
                     forward(5)
                 if kk == 2:
+                    spread(0, 1)
+                if kk == 3:
                     spread_end(0)
                     spread(1, 0)
-                if kk == 4:
-                    spread(1, 1)
+                    hop(1)
 
         def between():
             for kk in range(NB):
@@ -394,10 +402,12 @@
                         wait_top()
                         spread(0, 0)
                     if kk == 1:
-                        spread(0, 1)
                         wait_left()
-                    if kk > 0:
-                        hop(kk - 1)
+                        hop(0)
+                    if kk == 4:
+                        hop(2)
+                    if kk == 5:
+                        spread(1, 1)
 
         factor_diag(d_scr, v_scr, between)
         for kk in range(NB):
@@ -416,9 +426,72 @@
                         r = r - dot_t(w, u_scr[:lo, hi:])
                     u_scr[lo:hi, hi:] = dot(inverse, r)
 
+    pair = 2 * piece
+
+    def rows_of(which):
+        return pl.ds(pl.multiple_of(set_of(which) * pair, 8), pair)
+
+    def solve_left(group):
+        for which in group:
+            swap(which, 1 - core, set_of(which)).wait_recv()
+        raw = jnp.concatenate([left[pl.ds(2 * set_of(w), 2)].reshape(pair, B) for w in group], axis=0)
+        lh, ll = halves(raw)
+        dims = (((1,), (1,)), ((), ()))
+        for b in range(B // BLK):
+            lo, hi = b * BLK, (b + 1) * BLK
+            ih, il = i3[0, lo:hi, :hi], i3[1, lo:hi, :hi]
+            s = lax.dot_general(lh[:, :hi], ih, dims, preferred_element_type=F)
+            s += lax.dot_general(lh[:, :hi], il, dims, preferred_element_type=F)
+            s += lax.dot_general(ll[:, :hi], ih, dims, preferred_element_type=F)
+            for n, which in enumerate(group):
+                xl[rows_of(which), lo:hi] = s[n * pair : (n + 1) * pair]
+
+    hop(3)
+    high, low = halves(y_ref[...])
+    i3[0] = high
+    i3[1] = low
+    solve_left((0, 1, 5, 2, 6))
+
     spread_end(1)
-    for which in range(NZ):
-        swap(which, 1 - core, set_of(which)).wait_recv()
+    for g in range(NB):
+        high, low = halves(top[g].reshape(T, t3.shape[1]))
+        t3[g * T : g * T + T, :] = high
+        t3[B + g * T : B + g * T + T, :] = low
+    for b in reversed(range(B // BLK)):
+        lo, hi = b * BLK, (b + 1) * BLK
+        ih, il = i3[0, lo:hi, :hi], i3[1, lo:hi, :hi]
+        th, tl = t3[:hi, :], t3[B : B + hi, :]
+        s = jnp.dot(ih, th, preferred_element_type=F)
+        s += jnp.dot(ih, tl, preferred_element_type=F)
+        s += jnp.dot(il, th, preferred_element_type=F)
+        high, low = halves(s)
+        t3[lo:hi, :] = high
+        t3[B + lo : B + hi, :] = low
+    hop(4)
+    solve_left((3, 7, 4))
+    pltpu.make_async_copy(mob, buf, loc.at[2]).wait()
+
+    size = buf.shape[0] // STEPS
+
+    def store(n):
+        return pltpu.make_async_copy(
+            buf.at[n * size : (n + 1) * size, :], out.at[n * size : (n + 1) * size, :], os_.at[n]
+        )
+
+    for n in range(STEPS):
+        rows = slice(n * size, (n + 1) * size)
+        xh, xo = halves(xl[rows, :])
+        th, tl = t3[:B, :], t3[B:, :]
+        s = jnp.dot(xh, th, preferred_element_type=F)
+        s += jnp.dot(xh, tl, preferred_element_type=F)
+        s += jnp.dot(xo, th, preferred_element_type=F)
+        buf[rows, :] = buf[rows, :] - s
+
+        @pl.when(col < NB)
+        def _():
+            buf[rows, 0:T] = xl[rows, pl.ds(pl.multiple_of(jnp.minimum(col, NB - 1) * T, T), T)]
+
+        store(n).start()
 
     @pl.when(a_sender)
     def _():
@@ -479,121 +552,41 @@
         down(step, z).wait_send()
     for which in range(NZ):
         swap(which, core, set_of(which)).wait_send()
-
-
-def gather(mobility):
+    for n in range(STEPS):
+        store(n).wait()
+
+
+def on_device(mobility):
     rows, cols = mobility.shape
     D = pltpu.SemaphoreType.DMA
-    top, left, inverse = pl.pallas_call(
-        gather_kernel,
-        out_shape=(
-            jax.ShapeDtypeStruct((NB, NX, NY, T // R, cols), F),
-            jax.ShapeDtypeStruct((C, rows // C, B), F),
-            jax.ShapeDtypeStruct((B, B), F),
-        ),
+    return pl.pallas_call(
+        panel_kernel,
+        out_shape=jax.ShapeDtypeStruct(mobility.shape, F),
         in_specs=[pl.BlockSpec(memory_space=pl.ANY)],
-        out_specs=(
-            pl.BlockSpec(memory_space=pl.ANY),
-            pl.BlockSpec(memory_space=pl.ANY),
-            pl.BlockSpec(memory_space=pltpu.VMEM),
-        ),
+        out_specs=pl.BlockSpec(memory_space=pl.ANY),
         scratch_shapes=[
+            pltpu.VMEM((NB, NX, NY, T // R, cols), F),
+            pltpu.VMEM((C, rows // C, B), F),
+            pltpu.VMEM((B, B), F),
             pltpu.VMEM((2, B, B // 2), F),
             pltpu.VMEM((B, B), F),
             pltpu.VMEM((T, T), F),
             pltpu.VMEM((T, T), F),
+            pltpu.VMEM((rows, cols), F),
+            pltpu.VMEM((2, B, B), BF),
+            pltpu.VMEM((2 * B, cols), BF),
+            pltpu.VMEM((rows, B), F),
             D((NZ,)), D((NB // 2,)),
             D((NB // 2, NX)), D((NB, NB // 2, NY)), D((NB, NB // 2)),
             D((NB, NB // 2)), D((NB, NB // 2)),
-            D((R,)), D((NB,)), D((C,)), D((NB,)), D((2,)),
+            D((R,)), D((NB,)), D((C,)), D((NB,)), D((3,)),
             D((2, 2, 4)), D((2, 2, 4)),
-            D((4,)), D((4,)), D((3,)), D((3,)), D((NZ,)), D((NZ,)),
+            D((4,)), D((4,)), D((3,)), D((3,)), D((NZ,)), D((NZ,)), D((STEPS,)),
         ],
         compiler_params=pltpu.CompilerParams(
-            collective_id=0, has_side_effects=True, vmem_limit_bytes=32 << 20
+            collective_id=0, has_side_effects=True, vmem_limit_bytes=52 << 20
         ),
     )(mobility)
-    return top.reshape(B, cols), left.reshape(rows, B), inverse
-
-
-def halves(x):
-    high = x.astype(BF)
-    return high, (x - high.astype(F)).astype(BF)
-
-
-def update_kernel(steps, mob, left, top, inv, out, i3, t3, xl):
-    m = pl.program_id(0)
-    BLK = 256
-
-    @pl.when(m == 0)
-    def _():
-        high, low = halves(inv[...])
-        i3[0] = high
-        i3[1] = low
-        for b in range(B // BLK):
-            high, low = halves(top[b * BLK : (b + 1) * BLK, :])
-            t3[b * BLK : (b + 1) * BLK, :] = high
-            t3[B + b * BLK : B + (b + 1) * BLK, :] = low
-        for b in reversed(range(B // BLK)):
-            lo, hi = b * BLK, (b + 1) * BLK
-            ih, il = i3[0, lo:hi, :hi], i3[1, lo:hi, :hi]
-            th, tl = t3[:hi, :], t3[B : B + hi, :]
-            s = jnp.dot(ih, th, preferred_element_type=F)
-            s += jnp.dot(ih, tl, preferred_element_type=F)
-            s += jnp.dot(il, th, preferred_element_type=F)
-            high, low = halves(s)
-            t3[lo:hi, :] = high
-            t3[B + lo : B + hi, :] = low
-
-    lh, ll = halves(left[...])
-    dims = (((1,), (1,)), ((), ()))
-    for b in range(B // BLK):
-        lo, hi = b * BLK, (b + 1) * BLK
-        ih, il = i3[0, lo:hi, :hi], i3[1, lo:hi, :hi]
-        s = lax.dot_general(lh[:, :hi], ih, dims, preferred_element_type=F)
-        s += lax.dot_general(lh[:, :hi], il, dims, preferred_element_type=F)
-        s += lax.dot_general(ll[:, :hi], ih, dims, preferred_element_type=F)
-        xl[:, lo:hi] = s
-    xh, xo = halves(xl[...])
-    th, tl = t3[:B, :], t3[B:, :]
-    s = jnp.dot(xh, th, preferred_element_type=F)
-    s += jnp.dot(xh, tl, preferred_element_type=F)
-    s += jnp.dot(xo, th, preferred_element_type=F)
-    out[...] = mob[...] - s
-    col = lax.axis_index("col")
-
-    @pl.when(col < NB)
-    def _():
-        out[:, 0:T] = xl[:, pl.ds(pl.multiple_of(jnp.minimum(col, NB - 1) * T, T), T)]
-
-
-def update(mobility, left, top, inverse):
-    rows, cols = mobility.shape
-    steps = 6
-    tm = rows // steps
-    return pl.pallas_call(
-        functools.partial(update_kernel, steps),
-        grid=(steps,),
-        out_shape=jax.ShapeDtypeStruct(mobility.shape, F),
-        in_specs=[
-            pl.BlockSpec((tm, cols), lambda i: (i, 0)),
-            pl.BlockSpec((tm, B), lambda i: (i, 0)),
-            pl.BlockSpec((B, cols), lambda i: (0, 0)),
-            pl.BlockSpec((B, B), lambda i: (0, 0)),
-        ],
-        out_specs=pl.BlockSpec((tm, cols), lambda i: (i, 0)),
-        scratch_shapes=[
-            pltpu.VMEM((2, B, B), BF),
-            pltpu.VMEM((2 * B, cols), BF),
-            pltpu.VMEM((tm, B), F),
-        ],
-        compiler_params=pltpu.CompilerParams(vmem_limit_bytes=48 << 20),
-    )(mobility, left, top, inverse)
-
-
-def on_device(mobility):
-    top, left, inverse = gather(mobility)
-    return update(mobility, left, top, inverse)
 
 
 def solution(mesh):

time: 104 us -> 94.1 us (0.905); the launches traced: 102 us -> 93.9 us
  Pallas kernels: 97.8 us -> 88.7 us
    pallas_call x2 -> x1, Pallas kernels: 97.8 us -> 88.7 us  [on_device(): pl.pallas_call(panel_kernel, out_shape=jax.ShapeDtypeStruct(mobility.shap...]
    unnamed x4 -> x1, local copies, waits for them, and re-layouts: 4.24 us -> 5.23 us
where the time goes in v2:
time: 94.1 us; the launch traced here: 93.9 us
  Pallas kernels  88.7 us (94%)
  local copies, waits for them, and re-layouts  5.23 us (6%)
    pallas_call x1, Pallas kernels, on_device(): pl.pallas_call(panel_kernel, out_shape=jax.ShapeDtypeStruct(mobility.shap...  88.7 us
    unnamed x1, local copies, waits for them, and re-layouts  5.23 us

profile of v2, /device:TPU:1, one launch (start us, length us, event | category | flops | bytes accessed | tf_op | source)
XLA Modules:
  0.0 93.9 jit_solution(17962074506925498034)
XLA Ops:
  0.0 88.7 %shard_map.17 = f32[1152,1152]{1,0:T(8,128)} custom-call(f32[1152,1152]{1,0:T(8,128)} %mob.1), custom_call_target="tpu_custom_call" | custom-call | tf_op jit(solution)/shard_map/pallas_call | solution.py:562
  88.7 5.2 %copy.3 = f32[1152,1152]{1,0:T(8,128)} copy(f32[1152,1152]{1,0:T(8,128)} %shard_map.17) | data formatting | bytes 10616832

commit v3 on v2

--- a/solution.py
+++ b/solution.py
@@ -9,7 +9,7 @@
 T = 128
 NB = B // T
 BLK = 256
-STEPS = 3
+STEPS = 4
 NX, NY = 4, 4
 NZ = 8
 R = NX * NY
@@ -114,7 +114,7 @@
 
 
 def panel_kernel(
-    mob, out, top, left, y_ref, sq, u_scr, d_scr, v_scr, buf, i3, t3, xl,
+    mob, t3_out, xl_out, top, left, y_ref, sq, u_scr, d_scr, v_scr, i3, t3, xl,
     as_, ar, b1s, b2s, br, cs, cr, sts, str_, sls, slr, loc, ts, tr, us, ur, ds, dr, ws, wr, os_,
 ):
     row, col = lax.axis_index("row"), lax.axis_index("col")
@@ -254,8 +254,6 @@
     for r in range(NY):
         forward(r)
 
-    pltpu.make_async_copy(mob, buf, loc.at[2]).start()
-
     def swap_strip(r):
         for slot in range(NB // 2):
             @pl.when(2 * slot + core >= r)
@@ -295,14 +293,13 @@
             left_own().wait()
 
     H = NB // 2
-    PART = 640
 
     def tcopy(phase, axis, kind, at):
         src = (at + (0, 0, 3, 1)[kind]) % 4
         to = (at + (1, 3, 1, 3)[kind]) % 4
         if phase == 0:
-            lanes = (slice(None), slice(None), slice(0, PART), slice(PART, None))[kind]
-            ref = top.at[0:H, src, y, :, lanes] if axis == 0 else top.at[H:NB, x, src, :, lanes]
+            src, to = at, (at + (1, 3, 2)[kind]) % 4
+            ref = top.at[0:H, src, y] if axis == 0 else top.at[H:NB, x, src]
         else:
             part = (slice(None), slice(None), slice(0, 2), slice(2, 4))[kind]
             ref = top.at[0:H, part, src] if axis == 1 else top.at[H:NB, src, part]
@@ -311,57 +308,68 @@
 
     place = (x, y)
 
+    def kinds(phase):
+        return range(3) if phase == 0 else range(4)
+
+    def sender(phase, kind):
+        return (3, 1, 2)[kind] if phase == 0 else (3, 1, 3, 1)[kind]
+
     def spread(phase, step):
         for axis in range(2):
             if step == 1:
                 for kind in range(2):
-                    tcopy(phase, axis, kind, (place[axis] + (3, 1)[kind]) % 4).wait_recv()
-            for kind in range(2 * step, 2 * step + 2):
+                    tcopy(phase, axis, kind, (place[axis] + sender(phase, kind)) % 4).wait_recv()
+            for kind in range(3) if phase == 0 else range(2 * step, 2 * step + 2):
                 tcopy(phase, axis, kind, place[axis]).start()
 
     def spread_end(phase):
         for axis in range(2):
-            for kind in range(2, 4):
-                tcopy(phase, axis, kind, (place[axis] + (0, 0, 3, 1)[kind]) % 4).wait_recv()
+            for kind in range(3) if phase == 0 else range(2, 4):
+                tcopy(phase, axis, kind, (place[axis] + sender(phase, kind)) % 4).wait_recv()
 
     def spread_sent():
         for phase in range(2):
             for axis in range(2):
-                for kind in range(4):
+                for kind in kinds(phase):
                     tcopy(phase, axis, kind, place[axis]).wait_send()
+
+    HOPS = NZ // 2
+    part = piece // 16 * 8
 
     def up(step, at):
         ref = left.at[(at - step + NZ) % NZ * 2 + core]
+        if step == HOPS - 1:
+            ref = ref.at[0:part]
         return remote(ref, ref, us.at[step], ur.at[step], (row, (z + 1) % NZ * 2 + core))
 
     def down(step, at):
         ref = left.at[(at + step) % NZ * 2 + core]
+        if step == HOPS - 1:
+            ref = ref.at[part:piece]
         return remote(ref, ref, ds.at[step], dr.at[step], (row, (z + NZ - 1) % NZ * 2 + core))
 
-    UP, DOWN = 4, 3
 
     def swap(which, half, zz):
         ref = left.at[zz * 2 + half]
         return remote(ref, ref, ws.at[which], wr.at[which], (row, other))
 
     def set_of(which):
-        if which <= UP:
+        if which <= HOPS:
             return (z - which + NZ) % NZ
-        return (z + which - UP) % NZ
+        return (z + which - HOPS) % NZ
 
     def hop(step):
         if step > 0:
             up(step - 1, (z - 1 + NZ) % NZ).wait_recv()
-            swap(step, core, set_of(step)).start()
-            if step - 1 < DOWN:
-                down(step - 1, (z + 1) % NZ).wait_recv()
-                swap(UP + step, core, set_of(UP + step)).start()
-        else:
-            swap(0, core, z).start()
-        if step < UP:
+        if step < HOPS:
             up(step, z).start()
-        if step < DOWN:
+        if step > 0:
+            down(step - 1, (z + 1) % NZ).wait_recv()
+        if step < HOPS:
             down(step, z).start()
+        swap(step, core, set_of(step)).start()
+        if 0 < step < HOPS:
+            swap(HOPS + step, core, set_of(HOPS + step)).start()
 
     y_ref[...] = jnp.zeros_like(y_ref)
     swap_strip(0)
@@ -387,12 +395,10 @@
                 if kk == 0:
                     forward(4)
                     forward(5)
-                if kk == 2:
-                    spread(0, 1)
                 if kk == 3:
-                    spread_end(0)
-                    spread(1, 0)
                     hop(1)
+                if kk == 5:
+                    spread(1, 1)
 
         def between():
             for kk in range(NB):
@@ -404,10 +410,11 @@
                     if kk == 1:
                         wait_left()
                         hop(0)
+                    if kk == 2:
+                        spread_end(0)
+                        spread(1, 0)
                     if kk == 4:
                         hop(2)
-                    if kk == 5:
-                        spread(1, 1)
 
         factor_diag(d_scr, v_scr, between)
         for kk in range(NB):
@@ -446,11 +453,17 @@
             for n, which in enumerate(group):
                 xl[rows_of(which), lo:hi] = s[n * pair : (n + 1) * pair]
 
+    def save_left(which):
+        rows = rows_of(which)
+        return pltpu.make_async_copy(xl.at[rows, :], xl_out.at[rows, :], os_.at[which])
+
     hop(3)
     high, low = halves(y_ref[...])
     i3[0] = high
     i3[1] = low
     solve_left((0, 1, 5, 2, 6))
+    for which in (0, 1, 5, 2, 6):
+        save_left(which).start()
 
     spread_end(1)
     for g in range(NB):
@@ -467,31 +480,12 @@
         high, low = halves(s)
         t3[lo:hi, :] = high
         t3[B + lo : B + hi, :] = low
+    save_top = pltpu.make_async_copy(t3, t3_out, loc.at[2])
+    save_top.start()
     hop(4)
     solve_left((3, 7, 4))
-    pltpu.make_async_copy(mob, buf, loc.at[2]).wait()
-
-    size = buf.shape[0] // STEPS
-
-    def store(n):
-        return pltpu.make_async_copy(
-            buf.at[n * size : (n + 1) * size, :], out.at[n * size : (n + 1) * size, :], os_.at[n]
-        )
-
-    for n in range(STEPS):
-        rows = slice(n * size, (n + 1) * size)
-        xh, xo = halves(xl[rows, :])
-        th, tl = t3[:B, :], t3[B:, :]
-        s = jnp.dot(xh, th, preferred_element_type=F)
-        s += jnp.dot(xh, tl, preferred_element_type=F)
-        s += jnp.dot(xo, th, preferred_element_type=F)
-        buf[rows, :] = buf[rows, :] - s
-
-        @pl.when(col < NB)
-        def _():
-            buf[rows, 0:T] = xl[rows, pl.ds(pl.multiple_of(jnp.minimum(col, NB - 1) * T, T), T)]
-
-        store(n).start()
+    for which in (3, 7, 4):
+        save_left(which).start()
 
     @pl.when(a_sender)
     def _():
@@ -546,24 +540,23 @@
                 left_piece(i).wait_send()
 
     spread_sent()
-    for step in range(UP):
+    for step in range(HOPS):
         up(step, z).wait_send()
-    for step in range(DOWN):
         down(step, z).wait_send()
     for which in range(NZ):
         swap(which, core, set_of(which)).wait_send()
-    for n in range(STEPS):
-        store(n).wait()
-
-
-def on_device(mobility):
+        save_left(which).wait()
+    save_top.wait()
+
+
+def solve(mobility):
     rows, cols = mobility.shape
     D = pltpu.SemaphoreType.DMA
     return pl.pallas_call(
         panel_kernel,
-        out_shape=jax.ShapeDtypeStruct(mobility.shape, F),
+        out_shape=(jax.ShapeDtypeStruct((2 * B, cols), BF), jax.ShapeDtypeStruct((rows, B), F)),
         in_specs=[pl.BlockSpec(memory_space=pl.ANY)],
-        out_specs=pl.BlockSpec(memory_space=pl.ANY),
+        out_specs=(pl.BlockSpec(memory_space=pl.ANY), pl.BlockSpec(memory_space=pl.ANY)),
         scratch_shapes=[
             pltpu.VMEM((NB, NX, NY, T // R, cols), F),
             pltpu.VMEM((C, rows // C, B), F),
@@ -572,7 +565,6 @@
             pltpu.VMEM((B, B), F),
             pltpu.VMEM((T, T), F),
             pltpu.VMEM((T, T), F),
-            pltpu.VMEM((rows, cols), F),
             pltpu.VMEM((2, B, B), BF),
             pltpu.VMEM((2 * B, cols), BF),
             pltpu.VMEM((rows, B), F),
@@ -581,12 +573,44 @@
             D((NB, NB // 2)), D((NB, NB // 2)),
             D((R,)), D((NB,)), D((C,)), D((NB,)), D((3,)),
             D((2, 2, 4)), D((2, 2, 4)),
-            D((4,)), D((4,)), D((3,)), D((3,)), D((NZ,)), D((NZ,)), D((STEPS,)),
+            D((4,)), D((4,)), D((4,)), D((4,)), D((NZ,)), D((NZ,)), D((NZ,)),
         ],
         compiler_params=pltpu.CompilerParams(
             collective_id=0, has_side_effects=True, vmem_limit_bytes=52 << 20
         ),
     )(mobility)
+
+
+def update_kernel(mob, left, t3, out):
+    xh, xo = halves(left[...])
+    th, tl = t3[:B, :], t3[B:, :]
+    s = jnp.dot(xh, th, preferred_element_type=F)
+    s += jnp.dot(xh, tl, preferred_element_type=F)
+    s += jnp.dot(xo, th, preferred_element_type=F)
+    out[...] = mob[...] - s
+    col = lax.axis_index("col")
+
+    @pl.when(col < NB)
+    def _():
+        out[:, 0:T] = left[:, pl.ds(pl.multiple_of(jnp.minimum(col, NB - 1) * T, T), T)]
+
+
+def on_device(mobility):
+    rows, cols = mobility.shape
+    top, left = solve(mobility)
+    size = rows // STEPS
+    return pl.pallas_call(
+        update_kernel,
+        grid=(STEPS,),
+        out_shape=jax.ShapeDtypeStruct(mobility.shape, F),
+        in_specs=[
+            pl.BlockSpec((size, cols), lambda i: (i, 0)),
+            pl.BlockSpec((size, B), lambda i: (i, 0)),
+            pl.BlockSpec((2 * B, cols), lambda i: (0, 0)),
+        ],
+        out_specs=pl.BlockSpec((size, cols), lambda i: (i, 0)),
+        compiler_params=pltpu.CompilerParams(vmem_limit_bytes=56 << 20),
+    )(mobility, left, top)
 
 
 def solution(mesh):

time: 94.1 us -> 91.2 us (0.969)
  local copies, waits for them, and re-layouts: 5.23 us -> 0 us
  Pallas kernels: 88.7 us -> 91 us
    unnamed x1 -> x0, local copies, waits for them, and re-layouts: 5.23 us -> none
    pallas_call x1 -> x2, Pallas kernels: 88.7 us -> 91 us  [the longest x1 79 us: solve(): pl.pallas_call(panel_kernel, out_shape=(jax.ShapeDtypeStruct((2 * B, cols...]
where the time goes in v3:
time: 91.2 us; the launch traced here: 91 us
  Pallas kernels  91 us (100%)
    pallas_call x1, Pallas kernels, solve(): pl.pallas_call(panel_kernel, out_shape=(jax.ShapeDtypeStruct((2 * B, cols...  79 us
    pallas_call x1, Pallas kernels, on_device(): pl.pallas_call(update_kernel, grid=(STEPS,), out_shape=jax.ShapeDtypeStru...  12 us

profile of v3, /device:TPU:1, one launch (start us, length us, event | category | flops | bytes accessed | tf_op | source)
XLA Modules:
  0.0 91.0 jit_solution(8231901767933027565)
XLA Ops:
  0.0 79.0 %shard_map.17 = (bf16[1536,1152]{1,0:T(8,128)(2,1)}, f32[1152,768]{1,0:T(8,128)}) custom-call(f32[1152,1152]{1,0:T(8,128)} %mob.3), custom_call_target="tpu_custom_call" | custom-call | tf_op jit(solution)/shard_map/pallas_call | solution.py:555
  79.0 12.0 %shard_map.18 = f32[1152,1152]{1,0:T(8,128)} custom-call(f32[1152,1152]{1,0:T(8,128)} %mob.3, f32[1152,768]{1,0:T(8,128)} %get-tuple-element.7.left, bf16[1536,1152]{1,0:T(8,128)(2,1)} %get-tuple-element.8.t3), custom_call_target="tpu_custom_call" | custom-call | tf_op jit(solution)/shard_map/pallas_call | solution.py:602

commit v4 on v3

--- a/solution.py
+++ b/solution.py
@@ -483,7 +483,8 @@
     save_top = pltpu.make_async_copy(t3, t3_out, loc.at[2])
     save_top.start()
     hop(4)
-    solve_left((3, 7, 4))
+    solve_left((3, 7))
+    solve_left((4,))
     for which in (3, 7, 4):
         save_left(which).start()
 

time: 91.2 us -> 90.8 us (level)
  no operation moved by 1% of the time
where the time goes in v4:
time: 90.8 us; the launch traced here: 90.6 us
  Pallas kernels  90.6 us (100%)
    pallas_call x1, Pallas kernels, solve(): pl.pallas_call(panel_kernel, out_shape=(jax.ShapeDtypeStruct((2 * B, cols...  78.6 us
    pallas_call x1, Pallas kernels, on_device(): pl.pallas_call(update_kernel, grid=(STEPS,), out_shape=jax.ShapeDtypeStru...  12 us

profile of v4, /device:TPU:1, one launch (start us, length us, event | category | flops | bytes accessed | tf_op | source)
XLA Modules:
  0.0 90.6 jit_solution(12659247366281227666)
XLA Ops:
  0.0 78.6 %shard_map.17 = (bf16[1536,1152]{1,0:T(8,128)(2,1)}, f32[1152,768]{1,0:T(8,128)}) custom-call(f32[1152,1152]{1,0:T(8,128)} %mob.3), custom_call_target="tpu_custom_call" | custom-call | tf_op jit(solution)/shard_map/pallas_call | solution.py:556
  78.6 12.0 %shard_map.18 = f32[1152,1152]{1,0:T(8,128)} custom-call(f32[1152,1152]{1,0:T(8,128)} %mob.3, f32[1152,768]{1,0:T(8,128)} %get-tuple-element.7.left, bf16[1536,1152]{1,0:T(8,128)(2,1)} %get-tuple-element.8.t3), custom_call_target="tpu_custom_call" | custom-call | tf_op jit(solution)/shard_map/pallas_call | solution.py:603
